TPU v7x, 32 devices: a whole 2x2x4 slice. The times are simulated.
32 devices in a mesh: group: 4 (over x, core), seq: 8 (over z, y).
Axes of the slice: x: 2, y: 2, z: 4, core: 2. Of those that a mesh axis runs over, the one named last changes fastest.
Arguments:
- tokens: bfloat16 [4, 1024, 2048], P('group', 'seq'), may hold values from -6 to 6
- norm_gain: bfloat16 [2048], replicated, may hold values from 0.25 to 1.75
- w_qkv: bfloat16 [2048, 1920], P(('group', 'seq')), may hold values from -1.767767 to 1.767767
- prefix_kv: bfloat16 [4, 512, 640], P('group', 'seq'), may hold values from -12 to 12
- segments: int32 [4, 1024], P('group', 'seq'), may hold values from 0 to 3, never falling along the last dimension, each value on 1 to 512 neighbouring positions
Outputs:
- context: bfloat16 [4, 1024, 1280], P('group', 'seq')
Inputs may be any that keep to these rules, and one draw needn't show every extreme that they name: `segments`: within each group's 1024 suffix tokens the request numbers never fall; every request holds 1 to 512 tokens and one holds exactly 512.
All inputs are finite; a program needn't handle non-finite values.
Results may differ from a plain program's by a relative error of at most 0.0096.
Values may be sent and summed in bfloat16 or wider, within the bound.
No kernel may reach another device: no remote copies, remote signals or barrier semaphores. Data moves between devices by JAX's collectives and lax.ppermute only.
A program may use at most 64 MiB of HBM per device.

v0:
```python
import math
import jax
import jax.numpy as jnp
from jax import lax
from jax.sharding import PartitionSpec as P

HD = 64
QW = 1280
KVW = 320


def body(tokens, norm_gain, w_qkv, prefix_kv, segments):
    inputs = tokens[0]
    seg_ids = segments[0]
    row_count = inputs.shape[0]
    key_heads = KVW // HD
    repeats = QW // KVW
    values_f = inputs.astype(jnp.float32)
    mean_square = jnp.mean(values_f * values_f, axis=-1, keepdims=True)
    normed = (values_f * lax.rsqrt(mean_square + 1e-05) * norm_gain.astype(jnp.float32)).astype(
        jnp.bfloat16
    )
    folded = jnp.dot(
        normed,
        lax.all_gather(w_qkv, ("group", "seq"), axis=0, tiled=True),
        preferred_element_type=jnp.float32,
    )
    projected = folded.astype(jnp.bfloat16)
    queries = projected[:, :QW].reshape(row_count, key_heads, repeats, HD)
    local_kv = projected[:, QW:]

    def absorb(softmax_state, keyvals, visible):
        running_max, denominator, numerator = softmax_state
        key_count = keyvals.shape[0]
        key_part = keyvals[:, :KVW].reshape(key_count, key_heads, HD)
        value_part = keyvals[:, KVW:].reshape(key_count, key_heads, HD)
        scores = (
            jnp.einsum("tgrd,ngd->tgrn", queries, key_part, preferred_element_type=jnp.float32)
            * 0.125
        )
        if visible is not None:
            scores = jnp.where(visible[:, None, None, :], scores, jnp.float32(-1e30))
        new_max = jnp.maximum(running_max, jnp.max(scores, axis=-1))
        probability = jnp.exp(scores - new_max[..., None])
        if visible is not None:
            probability = jnp.where(visible[:, None, None, :], probability, jnp.float32(0.0))
        factor = jnp.exp(running_max - new_max)
        denominator = denominator * factor + jnp.sum(probability, axis=-1)
        numerator = numerator * factor[..., None] + jnp.einsum(
            "tgrn,ngd->tgrd",
            probability.astype(jnp.bfloat16),
            value_part,
            preferred_element_type=jnp.float32,
        )
        return (new_max, denominator, numerator)

    def sweep_keys(softmax_state, keyvals, key_seg, first_row, build):
        key_count = keyvals.shape[0]
        block_len = math.gcd(key_count, 512)
        if block_len == key_count:
            return absorb(softmax_state, keyvals, build(key_seg, first_row))

        def block_step(block_index, running):
            key_start = block_index * block_len
            keys_block = lax.dynamic_slice_in_dim(keyvals, key_start, block_len, 0)
            if key_seg is None:
                seg_block = None
            else:
                seg_block = lax.dynamic_slice_in_dim(key_seg, key_start, block_len, 0)
            return absorb(running, keys_block, build(seg_block, key_start))

        return lax.fori_loop(0, key_count // block_len, block_step, softmax_state)

    start_state = (
        jnp.full((row_count, key_heads, repeats), -1e30, jnp.float32),
        jnp.zeros((row_count, key_heads, repeats), jnp.float32),
        jnp.zeros((row_count, key_heads, repeats, HD), jnp.float32),
    )

    def open_rows(seg_block, key_start):
        return None

    softmax_state = sweep_keys(
        start_state,
        lax.all_gather(prefix_kv[0], "seq", axis=0, tiled=True),
        None,
        jnp.int32(0),
        open_rows,
    )
    query_pos = lax.axis_index("seq") * row_count + jnp.arange(row_count, dtype=jnp.int32)

    def causal_rows(seg_block, key_start):
        key_pos = key_start + jnp.arange(seg_block.shape[0], dtype=jnp.int32)
        return (seg_block[None, :] == seg_ids[:, None]) & (key_pos[None, :] <= query_pos[:, None])

    keyvals = lax.all_gather(local_kv, "seq", axis=0, tiled=True)
    key_seg = lax.all_gather(seg_ids, "seq", axis=0, tiled=True)
    softmax_state = sweep_keys(softmax_state, keyvals, key_seg, jnp.int32(0), causal_rows)
    running_max, denominator, numerator = softmax_state
    context = (numerator / denominator[..., None]).reshape(row_count, QW).astype(jnp.bfloat16)
    return context[None]


def solution(mesh):
    return jax.shard_map(
        body,
        mesh=mesh,
        in_specs=(
            P("group", "seq", None),
            P(),
            P(("group", "seq"), None),
            P("group", "seq", None),
            P("group", "seq"),
        ),
        out_specs=P("group", "seq", None),
        check_vma=False,
    )
```

profile of v0, /device:TPU:0, one launch (start us, length us, event | category | flops | bytes accessed | tf_op | source)
XLA Modules:
  0.0 169.5 jit_solution(7326391197680316243)
XLA Ops:
  6.5 0.0 all-gather.5.cloned.1.call-start
  6.5 0.7 all-gather.5.cloned.1.call-update
  7.3 0.0 all-gather.7.cloned.1.call-start
  7.3 0.7 convert_element_type.40
  8.0 1.2 fusion.30
  9.2 0.0 copy-start
  9.2 0.0 copy-start.1
  9.2 79.2 %all-gather.5.cloned.1.call-done = bf16[2048,1920]{1,0:T(8,128)(2,1)} async-done(((bf16[64,1920]{1,0:T(8,128)(2,1)}), bf16[2048,1920]{1,0:T(8,128)(2,1)}) %all-gather.5.cloned.1.call-update) | async-done | bytes 7864336 | tf_op jit(solution)/shard_map/all_gather | solution.py:25
  88.4 4.7 %convolution_convert_fusion = bf16[128,1920]{1,0:T(8,128)(2,1)S(1)} fusion(bf16[2048,1920]{1,0:T(8,128)(2,1)} %all-gather.5.cloned.1.call-done, bf16[1,128,2048]{2,1,0:T(8,128)(2,1)} %param.7, f32[2048]{0:T(1024)S(1)} %convert_element_type.40, f32[128]{0:T(128)S(1)} %add_rsqrt_fusion), kind=kOutput, calls=%fused_computation.27 | convolution fusion | flops 1007927296 | bytes 8888832 | tf_op jit(solution)/shard_map/dot_general | solution.py:23
  93.2 0.7 slice.35
  93.8 0.0 all-gather.7.cloned.1.call-update
  93.9 0.0 copy-done
  93.9 32.5 %all-gather = bf16[1,512,640]{2,1,0:T(8,128)(2,1)S(1)} all-gather(bf16[1,64,640]{2,1,0:T(8,128)(2,1)S(1)} %copy-done), channel_id=2, replica_groups=mesh['group'=4,'seq'=8] {'seq'}, dimensions={1}, use_global_device_ids=true | all-gather | bytes 737280 | tf_op jit(solution)/shard_map/all_gather | solution.py:85
  126.4 0.2 fusion.40
  126.6 0.2 copy.16
  126.8 0.2 copy.15
  126.9 0.0 copy-done.1
  127.0 19.3 %all-gather.1 = s32[1,1024]{1,0:T(1,128)S(1)} all-gather(s32[1,128]{1,0:T(1,128)S(1)} %copy-done.1), channel_id=3, replica_groups=mesh['group'=4,'seq'=8] {'seq'}, dimensions={1}, use_global_device_ids=true | all-gather | bytes 4608 | tf_op jit(solution)/shard_map/all_gather | solution.py:97
  146.3 0.2 copy.14
  146.5 1.0 bitcast_reduce_fusion
  147.5 1.3 fusion.19
  148.9 1.4 fusion.27
  150.3 0.0 all-gather.7.cloned.1.call-done
  150.3 11.3 %while.18 = (s32[]{:T(128)}, f32[128,5,4]{0,2,1:T(4,128)S(1)}, f32[128,5,4]{0,2,1:T(4,128)S(1)}, f32[128,5,4,64]{0,3,2,1:T(8,128)S(1)}, s32[1024]{0:T(1024)S(1)}...) while((s32[]{:T(128)}, f32[128,5,4]{0,2,1:T(4,128)S(1)}, ...), condition=%wide.region_6.7_spmd.clone, body=%wide.region_3.6_spmd.clone.sunk | while | flops 353113728 | bytes 21081812 | solution.py:72
  150.4 0.1 dynamic_slice.17
  150.4 0.2 compare_and_fusion.2
  150.6 1.4 fusion.60
  152.0 0.2 copy.29
  152.2 0.2 copy.30
  152.4 0.9 fusion.61
  153.3 1.2 fusion.62
  154.6 1.4 fusion.63
  156.0 0.1 dynamic_slice.17
  156.1 0.2 compare_and_fusion.2
  156.3 1.4 fusion.60
  157.7 0.2 copy.29
  157.9 0.2 copy.30
  158.0 0.9 fusion.61
  159.0 1.2 fusion.62
  160.2 1.4 fusion.63
  161.7 0.1 divide_convert_fusion
  161.7 0.9 copy.18
  (14 shorter events, 0.1 us)
Async XLA Ops:
  6.5 81.9 %all-gather.5.cloned.1.call-start = ((), (), s32[]{:S(2)}) async-start(), calls=%async_computation | async-start | bytes 8110080 | tf_op jit(solution)/shard_map/all_gather | solution.py:25
  7.3 143.1 %all-gather.7.cloned.1.call-start = ((), (), s32[]{:S(2)}) async-start(), calls=%async_computation.1 | async-start | bytes 1474560 | tf_op jit(solution)/shard_map/all_gather | solution.py:96
  9.2 84.6 %copy-start = (bf16[1,64,640]{2,1,0:T(8,128)(2,1)S(1)}, bf16[1,64,640]{2,1,0:T(8,128)(2,1)}, u32[]{:S(2)}) copy-start(bf16[1,64,640]{2,1,0:T(8,128)(2,1)} %param.10) | copy-start | bytes 245764
  9.2 117.7 %copy-start.1 = (s32[1,128]{1,0:T(1,128)S(1)}, s32[1,128]{1,0:T(1,128)}, u32[]{:S(2)}) copy-start(s32[1,128]{1,0:T(1,128)} %param.11) | copy-start | bytes 1540
Sparse Core Ops, SparseCore 0:
  10.3 78.1 all-gather.4
  94.0 42.5 all-gather.6
where the time goes:
time: 170 us; the launch traced here: 169 us
  waiting for transfers between devices  79.9 us (47%)
  blocking collectives  51.8 us (30%)
  between operations  13.5 us (8%)
  matrix products  11.8 us (7%)
  other arithmetic  6.27 us (4%)
  local copies, waits for them, and re-layouts  5.95 us (4%)
    all_gather x1, waiting for transfers between devices, body(): lax.all_gather(w_qkv, ('group', 'seq'), axis=0, tiled=True)  79.2 us
    all_gather x1, blocking collectives, body(): lax.all_gather(prefix_kv[0], 'seq', axis=0, tiled=True)  32.5 us
    all_gather x1, blocking collectives, body(): key_seg = lax.all_gather(seg_ids, 'seq', axis=0, tiled=True)  19.3 us
    dot_general x1, matrix products, body(): jnp.dot(normed, lax.all_gather(w_qkv, ('group', 'seq'), axis=0, tiled=Tru...  4.72 us
    dot_general x3, matrix products, absorb(): jnp.einsum('tgrn,ngd->tgrd', probability.astype(jnp.bfloat16), value_part...  4.22 us
    reduce_sum x3, other arithmetic, absorb(): denominator = denominator * factor + jnp.sum(probability, axis=-1)  3.76 us
  transfers between devices with their start and end apart: 2, of which 1 were waited for; matrix products, arithmetic and copies ran while one was open for 4% of the time, Pallas kernels for 0%

commit v1 on v0

--- a/solution.py
+++ b/solution.py
@@ -94,7 +94,15 @@
         return (seg_block[None, :] == seg_ids[:, None]) & (key_pos[None, :] <= query_pos[:, None])
 
     keyvals = lax.all_gather(local_kv, "seq", axis=0, tiled=True)
-    key_seg = lax.all_gather(seg_ids, "seq", axis=0, tiled=True)
+    n_blocks = lax.axis_size("seq")
+    e_next = seg_ids
+    newest = sorted(((d, (d + 1) % n_blocks) for d in range(n_blocks)))
+    pool = [e_next]
+    for h in tuple(range(1, n_blocks)):
+        e_next = lax.ppermute(e_next, "seq", newest)
+        pool.insert(0, e_next)
+    even = jnp.concatenate(pool, axis=0)
+    key_seg = jnp.roll(even, (lax.axis_index("seq") + 1) * seg_ids.shape[0], axis=0)
     softmax_state = sweep_keys(softmax_state, keyvals, key_seg, jnp.int32(0), causal_rows)
     running_max, denominator, numerator = softmax_state
     context = (numerator / denominator[..., None]).reshape(row_count, QW).astype(jnp.bfloat16)

time: 170 us -> 156 us (0.918)
  blocking collectives: 51.8 us -> 33.2 us
  starting transfers between devices: 0.04 us -> 3.08 us
    all_gather x1, waiting for transfers between devices: 79.2 us -> 8.48 us  [body(): lax.all_gather(w_qkv, ('group', 'seq'), axis=0, tiled=True)]
    all_gather x1, waiting for transfers between devices: 0.02 us -> 36.3 us  [body(): keyvals = lax.all_gather(local_kv, 'seq', axis=0, tiled=True)]
    ppermute x0 -> x7, waiting for transfers between devices: none -> 35 us  [body(): e_next = lax.ppermute(e_next, 'seq', newest)]
    all_gather x1 -> x0, blocking collectives: 19.3 us -> none  [body(): key_seg = lax.all_gather(seg_ids, 'seq', axis=0, tiled=True)]
    ppermute x0 -> x7, starting transfers between devices: none -> 3.04 us  [body(): e_next = lax.ppermute(e_next, 'seq', newest)]
  transfers between devices with their start and end apart: 2 -> 9, of which waited for: 1 -> 8; matrix products, arithmetic and copies ran while one was open for 4% -> 5% of each run, Pallas kernels for 0% -> 0%
where the time goes in v1:
time: 156 us; the launch traced here: 155 us
  waiting for transfers between devices  80.5 us (52%)
  blocking collectives  33.2 us (21%)
  between operations  13.6 us (9%)
  matrix products  11.8 us (8%)
  local copies, waits for them, and re-layouts  6.79 us (4%)
  other arithmetic  6.26 us (4%)
  starting transfers between devices  3.08 us (2%)
    all_gather x1, waiting for transfers between devices, body(): keyvals = lax.all_gather(local_kv, 'seq', axis=0, tiled=True)  36.3 us
    ppermute x7, waiting for transfers between devices, body(): e_next = lax.ppermute(e_next, 'seq', newest)  35 us
    all_gather x1, blocking collectives, body(): lax.all_gather(prefix_kv[0], 'seq', axis=0, tiled=True)  33.2 us
    all_gather x1, waiting for transfers between devices, body(): lax.all_gather(w_qkv, ('group', 'seq'), axis=0, tiled=True)  8.48 us
    dot_general x1, matrix products, body(): jnp.dot(normed, lax.all_gather(w_qkv, ('group', 'seq'), axis=0, tiled=Tru...  4.72 us
    dot_general x3, matrix products, absorb(): jnp.einsum('tgrn,ngd->tgrd', probability.astype(jnp.bfloat16), value_part...  4.22 us
    reduce_sum x3, other arithmetic, absorb(): denominator = denominator * factor + jnp.sum(probability, axis=-1)  3.76 us
  transfers between devices with their start and end apart: 9, of which 8 were waited for; matrix products, arithmetic and copies ran while one was open for 5% of the time, Pallas kernels for 0%

profile of v1, /device:TPU:0, one launch (start us, length us, event | category | flops | bytes accessed | tf_op | source)
XLA Modules:
  0.0 155.4 jit_solution(686209857335846115)
XLA Ops:
  6.5 0.0 all-gather.4.cloned.1.call-start
  6.5 0.7 all-gather.4.cloned.1.call-update
  7.3 0.0 all-gather.6.cloned.1.call-start
  7.3 3.0 %collective-permute-start = (s32[128]{0:T(128)}, s32[128]{0:T(128)S(1)}, u32[]{:S(2)}, u32[]{:S(2)}) collective-permute-start(s32[128]{0:T(128)} %bitcast.106), channel_id=1, source_target_pairs={{0,1},{1,2},{2,3},{3,4},{4,5},{5,6},{6,7},{7,0},{8,9},{9,10},{10,1... | collective-permute-start | bytes 1544 | tf_op jit(solution)/shard_map/ppermute | solution.py:102
  10.3 33.2 %all-gather = bf16[1,512,640]{2,1,0:T(8,128)(2,1)S(1)} all-gather(bf16[1,64,640]{2,1,0:T(8,128)(2,1)} %param.10), channel_id=2, replica_groups=mesh['group'=4,'seq'=8] {'seq'}, dimensions={1}, use_global_device_ids=true | all-gather | bytes 737280 | tf_op jit(solution)/shard_map/all_gather | solution.py:85
  43.6 0.0 collective-permute-done
  43.6 0.0 collective-permute-start.1
  43.6 0.2 fusion.40
  43.8 6.0 %collective-permute-done.1 = s32[128]{0:T(128)S(1)} collective-permute-done((s32[128]{0:T(128)S(1)}, s32[128]{0:T(128)S(1)}, u32[]{:S(2)}, u32[]{:S(2)}) %collective-permute-start.1) | collective-permute-done | bytes 544 | tf_op jit(solution)/shard_map/ppermute | solution.py:102
  49.8 0.0 collective-permute-start.2
  49.8 1.2 fusion.30
  51.0 5.0 %collective-permute-done.2 = s32[128]{0:T(128)S(1)} collective-permute-done((s32[128]{0:T(128)S(1)}, s32[128]{0:T(128)S(1)}, u32[]{:S(2)}, u32[]{:S(2)}) %collective-permute-start.2) | collective-permute-done | bytes 544 | tf_op jit(solution)/shard_map/ppermute | solution.py:102
  56.1 0.0 collective-permute-start.3
  56.1 6.2 %collective-permute-done.3 = s32[128]{0:T(128)S(1)} collective-permute-done((s32[128]{0:T(128)S(1)}, s32[128]{0:T(128)S(1)}, u32[]{:S(2)}, u32[]{:S(2)}) %collective-permute-start.3) | collective-permute-done | bytes 544 | tf_op jit(solution)/shard_map/ppermute | solution.py:102
  62.3 0.0 collective-permute-start.4
  62.3 6.2 %collective-permute-done.4 = s32[128]{0:T(128)S(1)} collective-permute-done((s32[128]{0:T(128)S(1)}, s32[128]{0:T(128)S(1)}, u32[]{:S(2)}, u32[]{:S(2)}) %collective-permute-start.4) | collective-permute-done | bytes 544 | tf_op jit(solution)/shard_map/ppermute | solution.py:102
  68.5 0.0 collective-permute-start.5
  68.5 6.2 %collective-permute-done.5 = s32[128]{0:T(128)S(1)} collective-permute-done((s32[128]{0:T(128)S(1)}, s32[128]{0:T(128)S(1)}, u32[]{:S(2)}, u32[]{:S(2)}) %collective-permute-start.5) | collective-permute-done | bytes 544 | tf_op jit(solution)/shard_map/ppermute | solution.py:102
  74.8 0.0 collective-permute-start.6
  74.8 0.7 convert_element_type.40
  75.5 0.2 copy.16
  75.7 0.2 copy.15
  75.8 5.2 %collective-permute-done.6 = s32[128]{0:T(128)S(1)} collective-permute-done((s32[128]{0:T(128)S(1)}, s32[128]{0:T(128)S(1)}, u32[]{:S(2)}, u32[]{:S(2)}) %collective-permute-start.6) | collective-permute-done | bytes 544 | tf_op jit(solution)/shard_map/ppermute | solution.py:102
  81.1 0.7 constant_dynamic-update-slice_fusion.8
  81.8 0.0 copy-start
  81.8 8.5 %all-gather.4.cloned.1.call-done = bf16[2048,1920]{1,0:T(8,128)(2,1)} async-done(((bf16[64,1920]{1,0:T(8,128)(2,1)}), bf16[2048,1920]{1,0:T(8,128)(2,1)}) %all-gather.4.cloned.1.call-update) | async-done | bytes 7864336 | tf_op jit(solution)/shard_map/all_gather | solution.py:25
  90.3 4.7 %convolution_convert_fusion = bf16[128,1920]{1,0:T(8,128)(2,1)S(1)} fusion(bf16[2048,1920]{1,0:T(8,128)(2,1)} %all-gather.4.cloned.1.call-done, bf16[1,128,2048]{2,1,0:T(8,128)(2,1)} %param.7, f32[2048]{0:T(1024)S(1)} %convert_element_type.40, f32[128]{0:T(128)S(1)} %add_rsqrt_fusion), kind=kOutput, calls=%fused_computation.27 | convolution fusion | flops 1007927296 | bytes 8888832 | tf_op jit(solution)/shard_map/dot_general | solution.py:23
  95.0 0.7 slice.35
  95.7 0.0 all-gather.6.cloned.1.call-update
  95.8 0.0 copy-done
  95.8 0.1 dynamic_slice.18
  95.9 0.2 copy.14
  96.1 1.0 bitcast_reduce_fusion
  97.1 1.3 fusion.19
  98.5 1.4 fusion.27
  99.9 36.3 %all-gather.6.cloned.1.call-done = bf16[1024,640]{1,0:T(8,128)(2,1)} async-done(((bf16[128,640]{1,0:T(8,128)(2,1)}), bf16[1024,640]{1,0:T(8,128)(2,1)}) %all-gather.6.cloned.1.call-update) | async-done | bytes 1310736 | tf_op jit(solution)/shard_map/all_gather | solution.py:96
  136.2 11.3 %while.18 = (s32[]{:T(128)}, f32[128,5,4]{0,2,1:T(4,128)S(1)}, f32[128,5,4]{0,2,1:T(4,128)S(1)}, f32[128,5,4,64]{0,3,2,1:T(8,128)S(1)}, s32[1024]{0:T(1024)S(1)}...) while((s32[]{:T(128)}, f32[128,5,4]{0,2,1:T(4,128)S(1)}, ...), condition=%wide.region_6.7_spmd.clone, body=%wide.region_3.6_spmd.clone.sunk | while | flops 353113728 | bytes 21081812 | solution.py:72
  136.2 0.1 dynamic_slice.22
  136.3 0.2 compare_and_fusion.2
  136.5 1.4 fusion.60
  137.9 0.2 copy.29
  138.1 0.2 copy.30
  138.2 0.9 fusion.61
  139.2 1.2 fusion.62
  140.4 1.4 fusion.63
  141.9 0.1 dynamic_slice.22
  142.0 0.2 compare_and_fusion.2
  142.2 1.4 fusion.60
  143.6 0.2 copy.29
  143.7 0.2 copy.30
  143.9 0.9 fusion.61
  144.8 1.2 fusion.62
  146.1 1.4 fusion.63
  147.5 0.1 divide_convert_fusion
  147.6 0.9 copy.18
  (30 shorter events, 0.2 us)
Async XLA Ops:
  6.5 83.7 %all-gather.4.cloned.1.call-start = ((), (), s32[]{:S(2)}) async-start(), calls=%async_computation | async-start | bytes 8110080 | tf_op jit(solution)/shard_map/all_gather | solution.py:25
  7.3 129.0 %all-gather.6.cloned.1.call-start = ((), (), s32[]{:S(2)}) async-start(), calls=%async_computation.1 | async-start | bytes 1474560 | tf_op jit(solution)/shard_map/all_gather | solution.py:96
  7.3 36.3 %collective-permute-start = (s32[128]{0:T(128)}, s32[128]{0:T(128)S(1)}, u32[]{:S(2)}, u32[]{:S(2)}) collective-permute-start(s32[128]{0:T(128)} %bitcast.106), channel_id=1, source_target_pairs={{0,1},{1,2},{2,3},{3,4},{4,5},{5,6},{6,7},{7,0},{8,9},{9,10},{10,1... | collective-permute-start | bytes 1544 | tf_op jit(solution)/shard_map/ppermute | solution.py:102
  43.6 6.2 %collective-permute-start.1 = (s32[128]{0:T(128)S(1)}, s32[128]{0:T(128)S(1)}, u32[]{:S(2)}, u32[]{:S(2)}) collective-permute-start(s32[128]{0:T(128)S(1)} %collective-permute-done), channel_id=1, source_target_pairs={{0,1},{1,2},{2,3},{3,4},{4,5},{5,6},{6,7},{7,0},{8,9},{9,10},{10,1... | collective-permute-start | bytes 1544 | tf_op jit(solution)/shard_map/ppermute | solution.py:102
  49.8 6.2 %collective-permute-start.2 = (s32[128]{0:T(128)S(1)}, s32[128]{0:T(128)S(1)}, u32[]{:S(2)}, u32[]{:S(2)}) collective-permute-start(s32[128]{0:T(128)S(1)} %collective-permute-done.1), channel_id=1, source_target_pairs={{0,1},{1,2},{2,3},{3,4},{4,5},{5,6},{6,7},{7,0},{8,9},{9,10},{10,1... | collective-permute-start | bytes 1544 | tf_op jit(solution)/shard_map/ppermute | solution.py:102
  56.1 6.2 %collective-permute-start.3 = (s32[128]{0:T(128)S(1)}, s32[128]{0:T(128)S(1)}, u32[]{:S(2)}, u32[]{:S(2)}) collective-permute-start(s32[128]{0:T(128)S(1)} %collective-permute-done.2), channel_id=1, source_target_pairs={{0,1},{1,2},{2,3},{3,4},{4,5},{5,6},{6,7},{7,0},{8,9},{9,10},{10,1... | collective-permute-start | bytes 1544 | tf_op jit(solution)/shard_map/ppermute | solution.py:102
  62.3 6.2 %collective-permute-start.4 = (s32[128]{0:T(128)S(1)}, s32[128]{0:T(128)S(1)}, u32[]{:S(2)}, u32[]{:S(2)}) collective-permute-start(s32[128]{0:T(128)S(1)} %collective-permute-done.3), channel_id=1, source_target_pairs={{0,1},{1,2},{2,3},{3,4},{4,5},{5,6},{6,7},{7,0},{8,9},{9,10},{10,1... | collective-permute-start | bytes 1544 | tf_op jit(solution)/shard_map/ppermute | solution.py:102
  68.5 6.2 %collective-permute-start.5 = (s32[128]{0:T(128)S(1)}, s32[128]{0:T(128)S(1)}, u32[]{:S(2)}, u32[]{:S(2)}) collective-permute-start(s32[128]{0:T(128)S(1)} %collective-permute-done.4), channel_id=1, source_target_pairs={{0,1},{1,2},{2,3},{3,4},{4,5},{5,6},{6,7},{7,0},{8,9},{9,10},{10,1... | collective-permute-start | bytes 1544 | tf_op jit(solution)/shard_map/ppermute | solution.py:102
  74.8 6.2 %collective-permute-start.6 = (s32[128]{0:T(128)S(1)}, s32[128]{0:T(128)S(1)}, u32[]{:S(2)}, u32[]{:S(2)}) collective-permute-start(s32[128]{0:T(128)S(1)} %collective-permute-done.5), channel_id=1, source_target_pairs={{0,1},{1,2},{2,3},{3,4},{4,5},{5,6},{6,7},{7,0},{8,9},{9,10},{10,1... | collective-permute-start | bytes 1544 | tf_op jit(solution)/shard_map/ppermute | solution.py:102
  81.8 14.0 %copy-start = (s32[1,128]{1,0:T(1,128)S(1)}, s32[1,128]{1,0:T(1,128)}, u32[]{:S(2)}) copy-start(s32[1,128]{1,0:T(1,128)} %param.11) | copy-start | bytes 1540
Sparse Core Ops, SparseCore 0:
  10.3 79.9 all-gather.3
  95.8 40.3 all-gather.5
